TPU v7x, 32 devices: a whole 2x2x4 slice. The times are simulated.
32 devices in a mesh: vel: 16 (over z, x, core), gx: 2 (over y).
Axes of the slice: x: 2, y: 2, z: 4, core: 2. Of those that a mesh axis runs over, the one named last changes fastest.
Arguments:
- distribution: float32 [4096, 8, 256], P('vel', 'gx'), as said below
Outputs:
- relaxed: float32 [4096, 8, 256], P('vel', 'gx')
Inputs may be any that keep to these rules, and one draw needn't show every extreme that they name: `distribution`: every entry is positive.
All inputs are finite; a program needn't handle non-finite values.
Results may differ from a plain program's by a relative error of at most 0.0003.
Values sent between devices are 32-bit elements; how exact they have to be, the bound alone decides.
A program may use at most 64 MiB of HBM per device.

v0:
```python
import math
import jax
import jax.numpy as jnp
from jax import lax
from jax.sharding import PartitionSpec as P

NV1 = 16
NZ = 16
COLLISIONS = 2
speed_limit = 4.0
time_step = 0.05
knudsen = 0.0125


def extended(value, sides, width):
    for axis, dim in sides:
        size, length = (lax.axis_size(axis), value.shape[dim])
        up = [(i, (i + 1) % size) for i in range(size)]
        down = [(j, i) for i, j in up]
        last = lax.slice_in_dim(value, length - width, length, axis=dim)
        leading = lax.slice_in_dim(value, 0, width, axis=dim)
        before = lax.ppermute(last, axis, up)
        after = lax.ppermute(leading, axis, down)
        value = jnp.concatenate([before, value, after], axis=dim)
    return value


def velocities(index):
    spacing = 2.0 * speed_limit / (NV1 - 1)
    first = index % NV1
    rest = index // NV1
    second = rest // NV1
    third = rest % NV1
    return [-speed_limit + spacing * part.astype(jnp.float32) for part in (first, second, third)]


def quad_weight():
    spacing = 2.0 * speed_limit / (NV1 - 1)
    return spacing**3 / (2.0 * math.pi) ** 1.5


def along_z(field, offset):
    zpos = jnp.arange(field.shape[-1], dtype=jnp.int32) % NZ
    main = jnp.roll(field, offset, -1)
    if offset > 0:
        other = jnp.roll(field, offset - NZ, -1)
        keep = zpos >= offset
    else:
        other = jnp.roll(field, offset + NZ, -1)
        keep = zpos < NZ + offset
    return jnp.where(keep, main, other)


def backward(field, minus_one, minus_two):
    return (3.0 * field - 4.0 * minus_one + minus_two) * 0.5


def forward(field, plus_one, plus_two):
    return (-3.0 * field + 4.0 * plus_one - plus_two) * 0.5


def upwind(field, comp, minus_one, minus_two, plus_one, plus_two):
    return jnp.where(
        comp > 0, backward(field, minus_one, minus_two), forward(field, plus_one, plus_two)
    )


def transverse(field, comp_y, comp_z):
    deriv_y = upwind(
        field,
        comp_y,
        jnp.roll(field, NZ, -1),
        jnp.roll(field, 2 * NZ, -1),
        jnp.roll(field, -NZ, -1),
        jnp.roll(field, -2 * NZ, -1),
    )
    deriv_z = upwind(
        field, comp_z, along_z(field, 1), along_z(field, 2), along_z(field, -1), along_z(field, -2)
    )
    return (deriv_y, deriv_z)


def along_x(field, comp_x):
    padded = extended(field, (("gx", 1),), 2)
    return upwind(field, comp_x, padded[:, 1:-3], padded[:, :-4], padded[:, 3:-1], padded[:, 4:])


def rate(field, comp_x, comp_y, comp_z):
    deriv_x = along_x(field, comp_x)
    deriv_y, deriv_z = transverse(field, comp_y, comp_z)
    return -(comp_x * deriv_x + comp_y * deriv_y + comp_z * deriv_z)


def advance(field, comp_x, comp_y, comp_z):
    first = field + time_step * rate(field, comp_x, comp_y, comp_z)
    second = 0.75 * field + 0.25 * (first + time_step * rate(first, comp_x, comp_y, comp_z))
    return field / 3.0 + 2.0 / 3.0 * (second + time_step * rate(second, comp_x, comp_y, comp_z))


def primitive(moments):
    rho = moments[0]
    vel_x = moments[1] / rho
    vel_y = moments[2] / rho
    vel_z = moments[3] / rho
    temp = (moments[4] / rho - (vel_x * vel_x + vel_y * vel_y + vel_z * vel_z)) / 3.0
    return jnp.stack([rho, vel_x, vel_y, vel_z, temp])


def maxwell(prims, comp_x, comp_y, comp_z):
    spread = (comp_x - prims[1]) ** 2 + (comp_y - prims[2]) ** 2 + (comp_z - prims[3]) ** 2
    return prims[0] * prims[4] ** (-1.5) * jnp.exp(-spread / (2.0 * prims[4]))


def separable_mass(prims):
    spacing = 2.0 * speed_limit / (NV1 - 1)
    points = -speed_limit + spacing * jnp.arange(NV1, dtype=jnp.float32)
    product = quad_weight() * prims[0] * prims[4] ** (-1.5)
    for which in (1, 2, 3):
        offset = points[:, None] - prims[which][None, :]
        product = product * jnp.sum(jnp.exp(-(offset * offset) / (2.0 * prims[4])), 0)
    return product


def collide(field, comp_x, comp_y, comp_z):
    count = field.shape[0]
    flat = field.reshape(count, -1)
    ones = jnp.ones_like(comp_x)
    table = (
        jnp.stack(
            [ones, comp_x, comp_y, comp_z, comp_x * comp_x + comp_y * comp_y + comp_z * comp_z]
        )
        * quad_weight()
    )
    local = jnp.dot(table, flat, precision=lax.Precision.HIGHEST)
    prims = primitive(lax.psum(local, "vel"))
    dense = maxwell(prims, comp_x[:, None], comp_y[:, None], comp_z[:, None])
    mass = separable_mass(prims)
    scale = prims[0] / mass
    rates = time_step * prims[0] * jnp.sqrt(prims[4]) / knudsen
    return ((flat + rates * (dense * scale)) / (1.0 + rates)).reshape(field.shape)


def on_device(distribution):
    count = distribution.shape[0]
    index = lax.axis_index("vel") * count + jnp.arange(count, dtype=jnp.int32)
    comp_x, comp_y, comp_z = velocities(index)
    field = distribution
    for step in range(COLLISIONS):
        field = advance(field, comp_x[:, None, None], comp_y[:, None, None], comp_z[:, None, None])
        field = collide(field, comp_x, comp_y, comp_z)
    return field


def solution(mesh):
    return jax.shard_map(
        on_device,
        mesh=mesh,
        in_specs=(P("vel", "gx", None),),
        out_specs=P("vel", "gx", None),
        check_vma=False,
    )
```

profile of v0, /device:TPU:0, one launch (start us, length us, event | category | flops | bytes accessed | tf_op | source)
XLA Modules:
  0.0 386.0 jit_solution(4824331936601160539)
XLA Ops:
  0.0 2.1 fusion.320
  2.9 3.0 collective-permute-start.1
  18.0 1.5 fusion.309
  21.3 1.5 fusion.310
  22.8 2.1 copy.101
  24.8 4.6 %collective-permute-done = f32[256,2,256]{2,0,1:T(8,128)} collective-permute-done((f32[256,2,256]{2,0,1:T(8,128)}, f32[256,2,256]{2,0,1:T(8,128)}, u32[]{:S(2)}, u32[]{:S(2)}) %collective-permute-start) | collective-permute-done | bytes 524320 | tf_op jit(solution)/shard_map/ppermute | solution.py:22
  29.4 2.0 copy.96
  31.4 7.4 %fusion.104 = f32[256,4,256]{0,2,1:T(8,128)S(1)} fusion(f32[256,4,256]{0,2,1:T(8,128)S(1)} %copy.92, f32[256,2,256]{0,2,1:T(8,128)} %copy.101, f32[256,2,256]{0,2,1:T(8,128)} %copy.96, f32[256,4,240]{0,2,1:T(8,128)} %get-tuple-element.188, f32[256,4,16]{0,2,1:T(8,128)S(1)} %get-tuple-element.190, f32[256,4,224]{0,2,1:T(8,128)} %get-tuple-element.184, ...), kind=kLoop, calls=%fused_computation.128 | loop fusion | flops 14942208 | bytes 15733504 | tf_op jit(solution)/shard_map/add | solution.py:95
  42.3 1.5 fusion.305
  43.8 1.5 fusion.300
  46.7 1.5 fusion.301
  50.2 1.7 collective-permute-start.3
  54.3 11.0 %collective-permute-done.3 = f32[256,2,256]{2,0,1:T(8,128)} collective-permute-done((f32[256,2,256]{2,0,1:T(8,128)}, f32[256,2,256]{2,0,1:T(8,128)}, u32[]{:S(2)}, u32[]{:S(2)}) %collective-permute-start.3) | collective-permute-done | bytes 524320 | tf_op jit(solution)/shard_map/ppermute | solution.py:23
  65.3 2.0 copy.130
  67.4 7.4 %collective-permute-done.2 = f32[256,2,256]{2,0,1:T(8,128)S(1)} collective-permute-done((f32[256,2,256]{2,0,1:T(8,128)S(1)}, f32[256,2,256]{2,0,1:T(8,128)S(1)}, u32[]{:S(2)}, u32[]{:S(2)}) %collective-permute-start.2) | collective-permute-done | bytes 524320 | tf_op jit(solution)/shard_map/ppermute | solution.py:22
  75.7 7.5 %fusion.87 = f32[256,4,256]{0,2,1:T(8,128)S(1)} fusion(f32[256,4,256]{0,2,1:T(8,128)S(1)} %fusion.104, f32[256,2,256]{0,2,1:T(8,128)} %copy.130, f32[256,2,256]{0,2,1:T(8,128)} %copy.128, f32[256,4,240]{0,2,1:T(8,128)} %get-tuple-element.162, f32[256,4,16]{0,2,1:T(8,128)S(1)} %get-tuple-element.164, f32[256,4,224]{0,2,1:T(8,128)} %get-tuple-element.158, ...), kind=kLoop, calls=%fused_computation.111 | loop fusion | flops 15728640 | bytes 16782080 | tf_op jit(solution)/shard_map/add | solution.py:96
  86.7 1.5 fusion.292
  88.2 1.5 fusion.287
  91.1 1.5 fusion.288
  98.7 11.0 %collective-permute-done.5 = f32[256,2,256]{2,0,1:T(8,128)} collective-permute-done((f32[256,2,256]{2,0,1:T(8,128)}, f32[256,2,256]{2,0,1:T(8,128)}, u32[]{:S(2)}, u32[]{:S(2)}) %collective-permute-start.5) | collective-permute-done | bytes 524320 | tf_op jit(solution)/shard_map/ppermute | solution.py:23
  109.7 2.0 copy.134
  111.8 6.5 %collective-permute-done.4 = f32[256,2,256]{2,0,1:T(8,128)S(1)} collective-permute-done((f32[256,2,256]{2,0,1:T(8,128)S(1)}, f32[256,2,256]{2,0,1:T(8,128)S(1)}, u32[]{:S(2)}, u32[]{:S(2)}) %collective-permute-start.4) | collective-permute-done | bytes 524320 | tf_op jit(solution)/shard_map/ppermute | solution.py:22
  119.3 7.5 %fusion.68 = f32[256,4,256]{0,2,1:T(8,128)S(1)} fusion(f32[256,4,256]{0,2,1:T(8,128)S(1)} %fusion.87, f32[256,2,256]{0,2,1:T(8,128)} %copy.134, f32[256,2,256]{0,2,1:T(8,128)} %copy.132, f32[256,4,240]{0,2,1:T(8,128)} %get-tuple-element.136, f32[256,4,16]{0,2,1:T(8,128)S(1)} %get-tuple-element.138, f32[256,4,224]{0,2,1:T(8,128)} %get-tuple-element.132, ...), kind=kLoop, calls=%fused_computation.92 | loop fusion | flops 15728640 | bytes 16782080 | tf_op jit(solution)/shard_map/add | solution.py:97
  127.8 58.6 %psum.14 = f32[5,1024]{1,0:T(8,128)S(1)} all-reduce(f32[5,1024]{1,0:T(8,128)S(1)} %fusion.208), channel_id=1, replica_groups=mesh['vel'=16,'gx'=2] {'vel'}, use_global_device_ids=true, to_apply=%region_0.1 | all-reduce | flops 5120 | bytes 40960 | tf_op jit(solution)/shard_map/psum | solution.py:135
  193.4 1.5 fusion.279
  195.0 1.5 fusion.274
  197.9 1.5 fusion.275
  201.4 1.5 collective-permute-start.7
  205.4 11.0 %collective-permute-done.7 = f32[256,2,256]{2,0,1:T(8,128)} collective-permute-done((f32[256,2,256]{2,0,1:T(8,128)}, f32[256,2,256]{2,0,1:T(8,128)}, u32[]{:S(2)}, u32[]{:S(2)}) %collective-permute-start.7) | collective-permute-done | bytes 524320 | tf_op jit(solution)/shard_map/ppermute | solution.py:23
  216.5 2.0 copy.138
  218.5 3.6 collective-permute-done.6
  223.1 7.3 %fusion.49 = f32[256,4,256]{0,2,1:T(8,128)S(1)} fusion(f32[256,4,256]{0,2,1:T(8,128)S(1)} %add_divide_fusion.1, f32[256,2,256]{0,2,1:T(8,128)} %copy.138, f32[256,2,256]{0,2,1:T(8,128)} %copy.136, f32[256,4,240]{0,2,1:T(8,128)} %get-tuple-element.110, f32[256,4,16]{0,2,1:T(8,128)S(1)} %get-tuple-element.112, f32[256,4,224]{0,2,1:T(8,128)} %get-tuple-element.106, ...), kind=kLoop, calls=%fused_computation.73 | loop fusion | flops 14942208 | bytes 15733504 | tf_op jit(solution)/shard_map/add | solution.py:95
  234.0 1.5 fusion.266
  235.5 1.5 fusion.261
  238.4 1.5 fusion.262
  241.9 1.5 collective-permute-start.9
  246.0 10.3 %collective-permute-done.9 = f32[256,2,256]{2,0,1:T(8,128)} collective-permute-done((f32[256,2,256]{2,0,1:T(8,128)}, f32[256,2,256]{2,0,1:T(8,128)}, u32[]{:S(2)}, u32[]{:S(2)}) %collective-permute-start.9) | collective-permute-done | bytes 524320 | tf_op jit(solution)/shard_map/ppermute | solution.py:23
  256.3 2.0 copy.142
  258.3 3.5 collective-permute-done.8
  262.8 8.2 %fusion.32 = f32[256,4,256]{0,2,1:T(8,128)S(1)} fusion(f32[256,4,256]{0,2,1:T(8,128)S(1)} %fusion.49, f32[256,2,256]{0,2,1:T(8,128)} %copy.142, f32[256,2,256]{0,2,1:T(8,128)} %copy.140, f32[256,4,240]{0,2,1:T(8,128)} %get-tuple-element.84, f32[256,4,16]{0,2,1:T(8,128)S(1)} %get-tuple-element.86, f32[256,4,224]{0,2,1:T(8,128)} %get-tuple-element.80, ...), kind=kLoop, calls=%fused_computation.56 | loop fusion | flops 19660800 | bytes 16814848 | tf_op jit(solution)/shard_map/add | solution.py:96
  274.5 1.5 fusion.253
  276.0 1.5 fusion.248
  282.4 1.5 collective-permute-start.11
  286.5 9.5 %collective-permute-done.11 = f32[256,2,256]{2,0,1:T(8,128)} collective-permute-done((f32[256,2,256]{2,0,1:T(8,128)}, f32[256,2,256]{2,0,1:T(8,128)}, u32[]{:S(2)}, u32[]{:S(2)}) %collective-permute-start.11) | collective-permute-done | bytes 524320 | tf_op jit(solution)/shard_map/ppermute | solution.py:23
  296.0 2.0 copy.146
  298.0 3.5 collective-permute-done.10
  302.5 8.4 %fusion.13 = f32[256,4,256]{0,2,1:T(8,128)S(1)} fusion(f32[256,4,256]{0,2,1:T(8,128)S(1)} %fusion.32, f32[256,2,256]{0,2,1:T(8,128)} %copy.146, f32[256,2,256]{0,2,1:T(8,128)} %copy.144, f32[256,4,240]{0,2,1:T(8,128)} %get-tuple-element.58, f32[256,4,16]{0,2,1:T(8,128)S(1)} %get-tuple-element.60, f32[256,4,224]{0,2,1:T(8,128)} %get-tuple-element.54, ...), kind=kLoop, calls=%fused_computation.37 | loop fusion | flops 19660800 | bytes 16814848 | tf_op jit(solution)/shard_map/add | solution.py:97
  311.9 69.8 %psum.15 = f32[5,1024]{1,0:T(8,128)S(1)} all-reduce(f32[5,1024]{1,0:T(8,128)S(1)} %fusion.206), channel_id=1, replica_groups=mesh['vel'=16,'gx'=2] {'vel'}, use_global_device_ids=true, to_apply=%region_4.5 | all-reduce | flops 5120 | bytes 40960 | tf_op jit(solution)/shard_map/psum | solution.py:135
  (174 shorter events, 79.4 us)
Async XLA Ops:
  2.1 9.2 %copy-start = (f32[256,4,256]{2,1,0:T(4,128)S(1)}, f32[256,4,256]{2,1,0:T(4,128)}, u32[]{:S(2)}) copy-start(f32[256,4,256]{2,1,0:T(4,128)} %param.1) | copy-start | bytes 3145732
  2.9 19.9 %collective-permute-start.1 = (f32[256,2,256]{2,0,1:T(8,128)}, f32[256,2,256]{2,0,1:T(8,128)}, u32[]{:S(2)}, u32[]{:S(2)}) collective-permute-start(f32[256,2,256]{2,0,1:T(8,128)} %copy.149), channel_id=1, source_target_pairs={{1,0},{0,1},{3,2},{2,3},{5,4},{4,5},{7,6},{6,7},{9,8},{8,9},{11,10... | collective-permute-start | bytes 1572872 | tf_op jit(solution)/shard_map/ppermute | solution.py:23
  6.7 22.6 %collective-permute-start = (f32[256,2,256]{2,0,1:T(8,128)}, f32[256,2,256]{2,0,1:T(8,128)}, u32[]{:S(2)}, u32[]{:S(2)}) collective-permute-start(f32[256,2,256]{2,0,1:T(8,128)} %copy.148), channel_id=1, source_target_pairs={{0,1},{1,0},{2,3},{3,2},{4,5},{5,4},{6,7},{7,6},{8,9},{9,8},{10,11... | collective-permute-start | bytes 1572872 | tf_op jit(solution)/shard_map/ppermute | solution.py:22
  19.5 1.1 copy-start.16
  19.5 1.1 copy-start.17
  19.5 1.1 copy-start.18
  19.5 1.1 copy-start.19
  49.2 2.7 copy-start.1
  50.2 15.1 %collective-permute-start.3 = (f32[256,2,256]{2,0,1:T(8,128)}, f32[256,2,256]{2,0,1:T(8,128)}, u32[]{:S(2)}, u32[]{:S(2)}) collective-permute-start(f32[256,2,256]{2,0,1:T(8,128)} %copy.129), channel_id=1, source_target_pairs={{1,0},{0,1},{3,2},{2,3},{5,4},{4,5},{7,6},{6,7},{9,8},{8,9},{11,10... | collective-permute-start | bytes 1572872 | tf_op jit(solution)/shard_map/ppermute | solution.py:23
  51.9 22.8 %collective-permute-start.2 = (f32[256,2,256]{2,0,1:T(8,128)S(1)}, f32[256,2,256]{2,0,1:T(8,128)S(1)}, u32[]{:S(2)}, u32[]{:S(2)}) collective-permute-start(f32[256,2,256]{2,0,1:T(8,128)S(1)} %copy-done.1), channel_id=1, source_target_pairs={{0,1},{1,0},{2,3},{3,2},{4,5},{5,4},{6,7},{7,6},{8,9},{9,8},{10,11... | collective-permute-start | bytes 1572872 | tf_op jit(solution)/shard_map/ppermute | solution.py:22
  93.6 2.5 copy-start.2
  94.6 15.1 %collective-permute-start.5 = (f32[256,2,256]{2,0,1:T(8,128)}, f32[256,2,256]{2,0,1:T(8,128)}, u32[]{:S(2)}, u32[]{:S(2)}) collective-permute-start(f32[256,2,256]{2,0,1:T(8,128)} %copy.133), channel_id=1, source_target_pairs={{1,0},{0,1},{3,2},{2,3},{5,4},{4,5},{7,6},{6,7},{9,8},{8,9},{11,10... | collective-permute-start | bytes 1572872 | tf_op jit(solution)/shard_map/ppermute | solution.py:23
  96.1 22.2 %collective-permute-start.4 = (f32[256,2,256]{2,0,1:T(8,128)S(1)}, f32[256,2,256]{2,0,1:T(8,128)S(1)}, u32[]{:S(2)}, u32[]{:S(2)}) collective-permute-start(f32[256,2,256]{2,0,1:T(8,128)S(1)} %copy-done.2), channel_id=1, source_target_pairs={{0,1},{1,0},{2,3},{3,2},{4,5},{5,4},{6,7},{7,6},{8,9},{9,8},{10,11... | collective-permute-start | bytes 1572872 | tf_op jit(solution)/shard_map/ppermute | solution.py:22
  126.8 60.8 %copy-start.20 = (f32[16]{0:T(128)S(1)}, f32[16]{0:T(128)}, u32[]{:S(2)}) copy-start(f32[16]{0:T(128)} %multiply_add_fusion.9) | copy-start | bytes 196
  126.8 61.8 %copy-start.6 = (f32[256]{0:T(256)S(1)}, f32[256]{0:T(256)}, u32[]{:S(2)}) copy-start(f32[256]{0:T(256)} %fusion.228) | copy-start | bytes 3076
  187.5 2.3 copy-start.8
  187.5 2.3 copy-start.9
  187.6 2.3 copy-start.10
  187.8 2.1 copy-start.11
  187.9 2.0 copy-start.12
  187.9 2.0 copy-start.13
  188.5 1.4 copy-start.14
  188.6 1.4 copy-start.15
  200.4 2.5 copy-start.3
  201.4 15.1 %collective-permute-start.7 = (f32[256,2,256]{2,0,1:T(8,128)}, f32[256,2,256]{2,0,1:T(8,128)}, u32[]{:S(2)}, u32[]{:S(2)}) collective-permute-start(f32[256,2,256]{2,0,1:T(8,128)} %copy.137), channel_id=1, source_target_pairs={{1,0},{0,1},{3,2},{2,3},{5,4},{4,5},{7,6},{6,7},{9,8},{8,9},{11,10... | collective-permute-start | bytes 1572872 | tf_op jit(solution)/shard_map/ppermute | solution.py:23
  202.9 19.2 %collective-permute-start.6 = (f32[256,2,256]{2,0,1:T(8,128)S(1)}, f32[256,2,256]{2,0,1:T(8,128)S(1)}, u32[]{:S(2)}, u32[]{:S(2)}) collective-permute-start(f32[256,2,256]{2,0,1:T(8,128)S(1)} %copy-done.3), channel_id=1, source_target_pairs={{0,1},{1,0},{2,3},{3,2},{4,5},{5,4},{6,7},{7,6},{8,9},{9,8},{10,11... | collective-permute-start | bytes 1572872 | tf_op jit(solution)/shard_map/ppermute | solution.py:22
  240.9 2.5 copy-start.4
  241.9 14.4 %collective-permute-start.9 = (f32[256,2,256]{2,0,1:T(8,128)}, f32[256,2,256]{2,0,1:T(8,128)}, u32[]{:S(2)}, u32[]{:S(2)}) collective-permute-start(f32[256,2,256]{2,0,1:T(8,128)} %copy.141), channel_id=1, source_target_pairs={{1,0},{0,1},{3,2},{2,3},{5,4},{4,5},{7,6},{6,7},{9,8},{8,9},{11,10... | collective-permute-start | bytes 1572872 | tf_op jit(solution)/shard_map/ppermute | solution.py:23
  243.4 18.4 %collective-permute-start.8 = (f32[256,2,256]{2,0,1:T(8,128)S(1)}, f32[256,2,256]{2,0,1:T(8,128)S(1)}, u32[]{:S(2)}, u32[]{:S(2)}) collective-permute-start(f32[256,2,256]{2,0,1:T(8,128)S(1)} %copy-done.4), channel_id=1, source_target_pairs={{0,1},{1,0},{2,3},{3,2},{4,5},{5,4},{6,7},{7,6},{8,9},{9,8},{10,11... | collective-permute-start | bytes 1572872 | tf_op jit(solution)/shard_map/ppermute | solution.py:22
  281.4 2.5 copy-start.5
  282.4 13.6 %collective-permute-start.11 = (f32[256,2,256]{2,0,1:T(8,128)}, f32[256,2,256]{2,0,1:T(8,128)}, u32[]{:S(2)}, u32[]{:S(2)}) collective-permute-start(f32[256,2,256]{2,0,1:T(8,128)} %copy.145), channel_id=1, source_target_pairs={{1,0},{0,1},{3,2},{2,3},{5,4},{4,5},{7,6},{6,7},{9,8},{8,9},{11,10... | collective-permute-start | bytes 1572872 | tf_op jit(solution)/shard_map/ppermute | solution.py:23
  283.9 17.6 %collective-permute-start.10 = (f32[256,2,256]{2,0,1:T(8,128)S(1)}, f32[256,2,256]{2,0,1:T(8,128)S(1)}, u32[]{:S(2)}, u32[]{:S(2)}) collective-permute-start(f32[256,2,256]{2,0,1:T(8,128)S(1)} %copy-done.5), channel_id=1, source_target_pairs={{0,1},{1,0},{2,3},{3,2},{4,5},{5,4},{6,7},{7,6},{8,9},{9,8},{10,11... | collective-permute-start | bytes 1572872 | tf_op jit(solution)/shard_map/ppermute | solution.py:22
  311.0 71.5 %copy-start.21 = (f32[16]{0:T(128)S(1)}, f32[16]{0:T(128)}, u32[]{:S(2)}) copy-start(f32[16]{0:T(128)} %multiply_add_fusion.9) | copy-start | bytes 196
  311.0 72.4 %copy-start.7 = (f32[256]{0:T(256)S(1)}, f32[256]{0:T(256)}, u32[]{:S(2)}) copy-start(f32[256]{0:T(256)} %fusion.228) | copy-start | bytes 3076
where the time goes:
time: 387 us; the launch traced here: 386 us
  blocking collectives  128 us (33%)
  local copies, waits for them, and re-layouts  104 us (27%)
  waiting for transfers between devices  81.9 us (21%)
  other arithmetic  56.3 us (15%)
  starting transfers between devices  13.1 us (3%)
    psum x2, blocking collectives, collide(): prims = primitive(lax.psum(local, 'vel'))  128 us
    ppermute x6, waiting for transfers between devices, extended(): after = lax.ppermute(leading, axis, down)  52.9 us
    ppermute x6, waiting for transfers between devices, extended(): before = lax.ppermute(last, axis, up)  29 us
    slice x24, local copies, waits for them, and re-layouts, along_z(): other = jnp.roll(field, offset + NZ, -1)  25.4 us
    slice x24, local copies, waits for them, and re-layouts, along_z(): main = jnp.roll(field, offset, -1)  24.6 us
    add x2, other arithmetic, advance(): field / 3.0  15.9 us
    add x2, other arithmetic, advance(): 0.75 * field  15.6 us
    add x2, other arithmetic, advance(): first = field + time_step * rate(field, comp_x, comp_y, comp_z)  14.7 us
  transfers between devices with their start and end apart: 12, of which 11 were waited for; matrix products, arithmetic and copies ran while one was open for 10% of the time, Pallas kernels for 0%

commit v1 on v0

--- a/solution.py
+++ b/solution.py
@@ -1,8 +1,10 @@
+import functools
 import math
 import jax
 import jax.numpy as jnp
 from jax import lax
 from jax.sharding import PartitionSpec as P
+from jax.lax import all_gather
 
 NV1 = 16
 NZ = 16
@@ -10,6 +12,14 @@
 speed_limit = 4.0
 time_step = 0.05
 knudsen = 0.0125
+
+
+def part_widths_all(x_in, lane_axis):
+    u_next = all_gather(x_in, lane_axis).sum(axis=0)
+    return u_next
+
+
+sides_produce = functools.partial(part_widths_all, lane_axis="vel")
 
 
 def extended(value, sides, width):
@@ -132,7 +142,7 @@
         * quad_weight()
     )
     local = jnp.dot(table, flat, precision=lax.Precision.HIGHEST)
-    prims = primitive(lax.psum(local, "vel"))
+    prims = primitive(sides_produce(local))
     dense = maxwell(prims, comp_x[:, None], comp_y[:, None], comp_z[:, None])
     mass = separable_mass(prims)
     scale = prims[0] / mass

time: 387 us -> 315 us (0.81)
  blocking collectives: 128 us -> 41.9 us
  waiting for transfers between devices: 81.9 us -> 96.4 us
    psum x2 -> x0, blocking collectives: 128 us -> none  [collide(): prims = primitive(lax.psum(local, 'vel'))]
    all_gather x0 -> x2, blocking collectives: none -> 41.9 us  [part_widths_all(): u_next = all_gather(x_in, lane_axis).sum(axis=0)]
    ppermute x6, waiting for transfers between devices: 29 us -> 41.3 us  [extended(): before = lax.ppermute(last, axis, up)]
  transfers between devices with their start and end apart: 12 -> 12, of which waited for: 11 -> 11; matrix products, arithmetic and copies ran while one was open for 10% -> 13% of each run, Pallas kernels for 0% -> 0%
where the time goes in v1:
time: 315 us; the launch traced here: 314 us
  local copies, waits for them, and re-layouts  104 us (33%)
  waiting for transfers between devices  96.4 us (31%)
  other arithmetic  56.4 us (18%)
  blocking collectives  41.9 us (13%)
  starting transfers between devices  13.1 us (4%)
    ppermute x6, waiting for transfers between devices, extended(): after = lax.ppermute(leading, axis, down)  55.1 us
    all_gather x2, blocking collectives, part_widths_all(): u_next = all_gather(x_in, lane_axis).sum(axis=0)  41.9 us
    ppermute x6, waiting for transfers between devices, extended(): before = lax.ppermute(last, axis, up)  41.3 us
    slice x24, local copies, waits for them, and re-layouts, along_z(): other = jnp.roll(field, offset + NZ, -1)  25.4 us
    slice x24, local copies, waits for them, and re-layouts, along_z(): main = jnp.roll(field, offset, -1)  24.6 us
    add x2, other arithmetic, advance(): field / 3.0  15.9 us
    add x2, other arithmetic, advance(): 0.75 * field  15.6 us
    add x2, other arithmetic, advance(): first = field + time_step * rate(field, comp_x, comp_y, comp_z)  14.7 us
  transfers between devices with their start and end apart: 12, of which 11 were waited for; matrix products, arithmetic and copies ran while one was open for 13% of the time, Pallas kernels for 0%

profile of v1, /device:TPU:0, one launch (start us, length us, event | category | flops | bytes accessed | tf_op | source)
XLA Modules:
  0.0 314.1 jit_solution(1132410315355761608)
XLA Ops:
  0.0 2.1 fusion.318
  2.9 3.0 collective-permute-start.1
  18.0 1.5 fusion.307
  21.3 1.5 fusion.308
  22.8 2.1 copy.101
  24.8 4.6 %collective-permute-done = f32[256,2,256]{2,0,1:T(8,128)} collective-permute-done((f32[256,2,256]{2,0,1:T(8,128)}, f32[256,2,256]{2,0,1:T(8,128)}, u32[]{:S(2)}, u32[]{:S(2)}) %collective-permute-start) | collective-permute-done | bytes 524320 | tf_op jit(solution)/shard_map/ppermute | solution.py:32
  29.4 2.0 copy.96
  31.4 7.4 %fusion.104 = f32[256,4,256]{0,2,1:T(8,128)S(1)} fusion(f32[256,4,256]{0,2,1:T(8,128)S(1)} %copy.92, f32[256,2,256]{0,2,1:T(8,128)} %copy.101, f32[256,2,256]{0,2,1:T(8,128)} %copy.96, f32[256,4,240]{0,2,1:T(8,128)} %get-tuple-element.188, f32[256,4,16]{0,2,1:T(8,128)S(1)} %get-tuple-element.190, f32[256,4,224]{0,2,1:T(8,128)} %get-tuple-element.184, ...), kind=kLoop, calls=%fused_computation.130 | loop fusion | flops 14942208 | bytes 15733504 | tf_op jit(solution)/shard_map/add | solution.py:105
  42.3 1.5 fusion.303
  43.8 1.5 fusion.298
  46.7 1.5 fusion.299
  50.2 1.7 collective-permute-start.3
  54.3 11.0 %collective-permute-done.3 = f32[256,2,256]{2,0,1:T(8,128)} collective-permute-done((f32[256,2,256]{2,0,1:T(8,128)}, f32[256,2,256]{2,0,1:T(8,128)}, u32[]{:S(2)}, u32[]{:S(2)}) %collective-permute-start.3) | collective-permute-done | bytes 524320 | tf_op jit(solution)/shard_map/ppermute | solution.py:33
  65.3 2.0 copy.130
  67.4 7.4 %collective-permute-done.2 = f32[256,2,256]{2,0,1:T(8,128)S(1)} collective-permute-done((f32[256,2,256]{2,0,1:T(8,128)S(1)}, f32[256,2,256]{2,0,1:T(8,128)S(1)}, u32[]{:S(2)}, u32[]{:S(2)}) %collective-permute-start.2) | collective-permute-done | bytes 524320 | tf_op jit(solution)/shard_map/ppermute | solution.py:32
  75.7 7.5 %fusion.87 = f32[256,4,256]{0,2,1:T(8,128)S(1)} fusion(f32[256,4,256]{0,2,1:T(8,128)S(1)} %fusion.104, f32[256,2,256]{0,2,1:T(8,128)} %copy.130, f32[256,2,256]{0,2,1:T(8,128)} %copy.128, f32[256,4,240]{0,2,1:T(8,128)} %get-tuple-element.162, f32[256,4,16]{0,2,1:T(8,128)S(1)} %get-tuple-element.164, f32[256,4,224]{0,2,1:T(8,128)} %get-tuple-element.158, ...), kind=kLoop, calls=%fused_computation.113 | loop fusion | flops 15728640 | bytes 16782080 | tf_op jit(solution)/shard_map/add | solution.py:106
  86.7 1.5 fusion.290
  88.2 1.5 fusion.285
  91.1 1.5 fusion.286
  98.7 11.0 %collective-permute-done.5 = f32[256,2,256]{2,0,1:T(8,128)} collective-permute-done((f32[256,2,256]{2,0,1:T(8,128)}, f32[256,2,256]{2,0,1:T(8,128)}, u32[]{:S(2)}, u32[]{:S(2)}) %collective-permute-start.5) | collective-permute-done | bytes 524320 | tf_op jit(solution)/shard_map/ppermute | solution.py:33
  109.7 2.0 copy.134
  111.8 6.5 %collective-permute-done.4 = f32[256,2,256]{2,0,1:T(8,128)S(1)} collective-permute-done((f32[256,2,256]{2,0,1:T(8,128)S(1)}, f32[256,2,256]{2,0,1:T(8,128)S(1)}, u32[]{:S(2)}, u32[]{:S(2)}) %collective-permute-start.4) | collective-permute-done | bytes 524320 | tf_op jit(solution)/shard_map/ppermute | solution.py:32
  119.3 7.5 %fusion.68 = f32[256,4,256]{0,2,1:T(8,128)S(1)} fusion(f32[256,4,256]{0,2,1:T(8,128)S(1)} %fusion.87, f32[256,2,256]{0,2,1:T(8,128)} %copy.134, f32[256,2,256]{0,2,1:T(8,128)} %copy.132, f32[256,4,240]{0,2,1:T(8,128)} %get-tuple-element.136, f32[256,4,16]{0,2,1:T(8,128)S(1)} %get-tuple-element.138, f32[256,4,224]{0,2,1:T(8,128)} %get-tuple-element.132, ...), kind=kLoop, calls=%fused_computation.94 | loop fusion | flops 15728640 | bytes 16782080 | tf_op jit(solution)/shard_map/add | solution.py:107
  127.8 23.1 %all-gather.2 = f32[16,5,1024]{2,1,0:T(8,128)S(1)} all-gather(f32[1,5,1024]{2,1,0:T(8,128)S(1)} %convolution_bitcast_fusion.1), channel_id=2, replica_groups=mesh['vel'=16,'gx'=2] {'vel'}, dimensions={0}, use_global_device_ids=true | all-gather | bytes 348160 | tf_op jit(solution)/shard_map/all_gather | solution.py:18
  158.1 1.5 fusion.277
  159.6 1.5 fusion.272
  162.5 1.5 fusion.273
  166.0 1.5 collective-permute-start.7
  170.1 11.0 %collective-permute-done.7 = f32[256,2,256]{2,0,1:T(8,128)} collective-permute-done((f32[256,2,256]{2,0,1:T(8,128)}, f32[256,2,256]{2,0,1:T(8,128)}, u32[]{:S(2)}, u32[]{:S(2)}) %collective-permute-start.7) | collective-permute-done | bytes 524320 | tf_op jit(solution)/shard_map/ppermute | solution.py:33
  181.1 2.0 copy.138
  183.1 8.5 %collective-permute-done.6 = f32[256,2,256]{2,0,1:T(8,128)S(1)} collective-permute-done((f32[256,2,256]{2,0,1:T(8,128)S(1)}, f32[256,2,256]{2,0,1:T(8,128)S(1)}, u32[]{:S(2)}, u32[]{:S(2)}) %collective-permute-start.6) | collective-permute-done | bytes 524320 | tf_op jit(solution)/shard_map/ppermute | solution.py:32
  192.6 7.3 %fusion.49 = f32[256,4,256]{0,2,1:T(8,128)S(1)} fusion(f32[256,4,256]{0,2,1:T(8,128)S(1)} %add_divide_fusion.1, f32[256,2,256]{0,2,1:T(8,128)} %copy.138, f32[256,2,256]{0,2,1:T(8,128)} %copy.136, f32[256,4,240]{0,2,1:T(8,128)} %get-tuple-element.110, f32[256,4,16]{0,2,1:T(8,128)S(1)} %get-tuple-element.112, f32[256,4,224]{0,2,1:T(8,128)} %get-tuple-element.106, ...), kind=kLoop, calls=%fused_computation.75 | loop fusion | flops 14942208 | bytes 15733504 | tf_op jit(solution)/shard_map/add | solution.py:105
  203.5 1.5 fusion.264
  205.0 1.5 fusion.259
  207.9 1.5 fusion.260
  211.4 1.5 collective-permute-start.9
  215.5 11.0 %collective-permute-done.9 = f32[256,2,256]{2,0,1:T(8,128)} collective-permute-done((f32[256,2,256]{2,0,1:T(8,128)}, f32[256,2,256]{2,0,1:T(8,128)}, u32[]{:S(2)}, u32[]{:S(2)}) %collective-permute-start.9) | collective-permute-done | bytes 524320 | tf_op jit(solution)/shard_map/ppermute | solution.py:33
  226.5 2.0 copy.142
  228.5 7.6 %collective-permute-done.8 = f32[256,2,256]{2,0,1:T(8,128)S(1)} collective-permute-done((f32[256,2,256]{2,0,1:T(8,128)S(1)}, f32[256,2,256]{2,0,1:T(8,128)S(1)}, u32[]{:S(2)}, u32[]{:S(2)}) %collective-permute-start.8) | collective-permute-done | bytes 524320 | tf_op jit(solution)/shard_map/ppermute | solution.py:32
  237.1 8.2 %fusion.32 = f32[256,4,256]{0,2,1:T(8,128)S(1)} fusion(f32[256,4,256]{0,2,1:T(8,128)S(1)} %fusion.49, f32[256,2,256]{0,2,1:T(8,128)} %copy.142, f32[256,2,256]{0,2,1:T(8,128)} %copy.140, f32[256,4,240]{0,2,1:T(8,128)} %get-tuple-element.84, f32[256,4,16]{0,2,1:T(8,128)S(1)} %get-tuple-element.86, f32[256,4,224]{0,2,1:T(8,128)} %get-tuple-element.80, ...), kind=kLoop, calls=%fused_computation.58 | loop fusion | flops 19660800 | bytes 16814848 | tf_op jit(solution)/shard_map/add | solution.py:106
  248.8 1.5 fusion.251
  250.3 1.5 fusion.246
  256.7 1.5 collective-permute-start.11
  260.8 11.0 %collective-permute-done.11 = f32[256,2,256]{2,0,1:T(8,128)} collective-permute-done((f32[256,2,256]{2,0,1:T(8,128)}, f32[256,2,256]{2,0,1:T(8,128)}, u32[]{:S(2)}, u32[]{:S(2)}) %collective-permute-start.11) | collective-permute-done | bytes 524320 | tf_op jit(solution)/shard_map/ppermute | solution.py:33
  271.8 2.0 copy.146
  273.9 6.8 %collective-permute-done.10 = f32[256,2,256]{2,0,1:T(8,128)S(1)} collective-permute-done((f32[256,2,256]{2,0,1:T(8,128)S(1)}, f32[256,2,256]{2,0,1:T(8,128)S(1)}, u32[]{:S(2)}, u32[]{:S(2)}) %collective-permute-start.10) | collective-permute-done | bytes 524320 | tf_op jit(solution)/shard_map/ppermute | solution.py:32
  281.6 8.4 %fusion.13 = f32[256,4,256]{0,2,1:T(8,128)S(1)} fusion(f32[256,4,256]{0,2,1:T(8,128)S(1)} %fusion.32, f32[256,2,256]{0,2,1:T(8,128)} %copy.146, f32[256,2,256]{0,2,1:T(8,128)} %copy.144, f32[256,4,240]{0,2,1:T(8,128)} %get-tuple-element.58, f32[256,4,16]{0,2,1:T(8,128)S(1)} %get-tuple-element.60, f32[256,4,224]{0,2,1:T(8,128)} %get-tuple-element.54, ...), kind=kLoop, calls=%fused_computation.39 | loop fusion | flops 19660800 | bytes 16814848 | tf_op jit(solution)/shard_map/add | solution.py:107
  291.1 18.7 %all-gather.3 = f32[16,5,1024]{2,1,0:T(8,128)S(1)} all-gather(f32[1,5,1024]{2,1,0:T(8,128)S(1)} %convolution_bitcast_fusion), channel_id=3, replica_groups=mesh['vel'=16,'gx'=2] {'vel'}, dimensions={0}, use_global_device_ids=true | all-gather | bytes 348160 | tf_op jit(solution)/shard_map/all_gather | solution.py:18
  (176 shorter events, 79.5 us)
Async XLA Ops:
  2.1 9.2 %copy-start = (f32[256,4,256]{2,1,0:T(4,128)S(1)}, f32[256,4,256]{2,1,0:T(4,128)}, u32[]{:S(2)}) copy-start(f32[256,4,256]{2,1,0:T(4,128)} %param.1) | copy-start | bytes 3145732
  2.9 19.9 %collective-permute-start.1 = (f32[256,2,256]{2,0,1:T(8,128)}, f32[256,2,256]{2,0,1:T(8,128)}, u32[]{:S(2)}, u32[]{:S(2)}) collective-permute-start(f32[256,2,256]{2,0,1:T(8,128)} %copy.149), channel_id=1, source_target_pairs={{1,0},{0,1},{3,2},{2,3},{5,4},{4,5},{7,6},{6,7},{9,8},{8,9},{11,10... | collective-permute-start | bytes 1572872 | tf_op jit(solution)/shard_map/ppermute | solution.py:33
  6.7 22.6 %collective-permute-start = (f32[256,2,256]{2,0,1:T(8,128)}, f32[256,2,256]{2,0,1:T(8,128)}, u32[]{:S(2)}, u32[]{:S(2)}) collective-permute-start(f32[256,2,256]{2,0,1:T(8,128)} %copy.148), channel_id=1, source_target_pairs={{0,1},{1,0},{2,3},{3,2},{4,5},{5,4},{6,7},{7,6},{8,9},{9,8},{10,11... | collective-permute-start | bytes 1572872 | tf_op jit(solution)/shard_map/ppermute | solution.py:32
  19.5 1.1 copy-start.16
  19.5 1.1 copy-start.17
  19.5 1.1 copy-start.18
  19.5 1.1 copy-start.19
  49.2 2.7 copy-start.1
  50.2 15.1 %collective-permute-start.3 = (f32[256,2,256]{2,0,1:T(8,128)}, f32[256,2,256]{2,0,1:T(8,128)}, u32[]{:S(2)}, u32[]{:S(2)}) collective-permute-start(f32[256,2,256]{2,0,1:T(8,128)} %copy.129), channel_id=1, source_target_pairs={{1,0},{0,1},{3,2},{2,3},{5,4},{4,5},{7,6},{6,7},{9,8},{8,9},{11,10... | collective-permute-start | bytes 1572872 | tf_op jit(solution)/shard_map/ppermute | solution.py:33
  51.9 22.8 %collective-permute-start.2 = (f32[256,2,256]{2,0,1:T(8,128)S(1)}, f32[256,2,256]{2,0,1:T(8,128)S(1)}, u32[]{:S(2)}, u32[]{:S(2)}) collective-permute-start(f32[256,2,256]{2,0,1:T(8,128)S(1)} %copy-done.1), channel_id=1, source_target_pairs={{0,1},{1,0},{2,3},{3,2},{4,5},{5,4},{6,7},{7,6},{8,9},{9,8},{10,11... | collective-permute-start | bytes 1572872 | tf_op jit(solution)/shard_map/ppermute | solution.py:32
  93.6 2.5 copy-start.2
  94.6 15.1 %collective-permute-start.5 = (f32[256,2,256]{2,0,1:T(8,128)}, f32[256,2,256]{2,0,1:T(8,128)}, u32[]{:S(2)}, u32[]{:S(2)}) collective-permute-start(f32[256,2,256]{2,0,1:T(8,128)} %copy.133), channel_id=1, source_target_pairs={{1,0},{0,1},{3,2},{2,3},{5,4},{4,5},{7,6},{6,7},{9,8},{8,9},{11,10... | collective-permute-start | bytes 1572872 | tf_op jit(solution)/shard_map/ppermute | solution.py:33
  96.1 22.2 %collective-permute-start.4 = (f32[256,2,256]{2,0,1:T(8,128)S(1)}, f32[256,2,256]{2,0,1:T(8,128)S(1)}, u32[]{:S(2)}, u32[]{:S(2)}) collective-permute-start(f32[256,2,256]{2,0,1:T(8,128)S(1)} %copy-done.2), channel_id=1, source_target_pairs={{0,1},{1,0},{2,3},{3,2},{4,5},{5,4},{6,7},{7,6},{8,9},{9,8},{10,11... | collective-permute-start | bytes 1572872 | tf_op jit(solution)/shard_map/ppermute | solution.py:32
  126.8 25.5 %copy-start.20 = (f32[16]{0:T(128)S(1)}, f32[16]{0:T(128)}, u32[]{:S(2)}) copy-start(f32[16]{0:T(128)} %multiply_add_fusion.9) | copy-start | bytes 196
  126.8 26.4 %copy-start.6 = (f32[256]{0:T(256)S(1)}, f32[256]{0:T(256)}, u32[]{:S(2)}) copy-start(f32[256]{0:T(256)} %fusion.226) | copy-start | bytes 3076
  152.1 2.3 copy-start.8
  152.2 2.3 copy-start.9
  152.2 2.3 copy-start.10
  152.5 2.1 copy-start.11
  152.5 2.0 copy-start.12
  152.5 2.0 copy-start.13
  153.2 1.4 copy-start.14
  153.2 1.4 copy-start.15
  165.0 2.5 copy-start.3
  166.0 15.1 %collective-permute-start.7 = (f32[256,2,256]{2,0,1:T(8,128)}, f32[256,2,256]{2,0,1:T(8,128)}, u32[]{:S(2)}, u32[]{:S(2)}) collective-permute-start(f32[256,2,256]{2,0,1:T(8,128)} %copy.137), channel_id=1, source_target_pairs={{1,0},{0,1},{3,2},{2,3},{5,4},{4,5},{7,6},{6,7},{9,8},{8,9},{11,10... | collective-permute-start | bytes 1572872 | tf_op jit(solution)/shard_map/ppermute | solution.py:33
  167.5 24.1 %collective-permute-start.6 = (f32[256,2,256]{2,0,1:T(8,128)S(1)}, f32[256,2,256]{2,0,1:T(8,128)S(1)}, u32[]{:S(2)}, u32[]{:S(2)}) collective-permute-start(f32[256,2,256]{2,0,1:T(8,128)S(1)} %copy-done.3), channel_id=1, source_target_pairs={{0,1},{1,0},{2,3},{3,2},{4,5},{5,4},{6,7},{7,6},{8,9},{9,8},{10,11... | collective-permute-start | bytes 1572872 | tf_op jit(solution)/shard_map/ppermute | solution.py:32
  210.4 2.5 copy-start.4
  211.4 15.1 %collective-permute-start.9 = (f32[256,2,256]{2,0,1:T(8,128)}, f32[256,2,256]{2,0,1:T(8,128)}, u32[]{:S(2)}, u32[]{:S(2)}) collective-permute-start(f32[256,2,256]{2,0,1:T(8,128)} %copy.141), channel_id=1, source_target_pairs={{1,0},{0,1},{3,2},{2,3},{5,4},{4,5},{7,6},{6,7},{9,8},{8,9},{11,10... | collective-permute-start | bytes 1572872 | tf_op jit(solution)/shard_map/ppermute | solution.py:33
  212.9 23.2 %collective-permute-start.8 = (f32[256,2,256]{2,0,1:T(8,128)S(1)}, f32[256,2,256]{2,0,1:T(8,128)S(1)}, u32[]{:S(2)}, u32[]{:S(2)}) collective-permute-start(f32[256,2,256]{2,0,1:T(8,128)S(1)} %copy-done.4), channel_id=1, source_target_pairs={{0,1},{1,0},{2,3},{3,2},{4,5},{5,4},{6,7},{7,6},{8,9},{9,8},{10,11... | collective-permute-start | bytes 1572872 | tf_op jit(solution)/shard_map/ppermute | solution.py:32
  255.7 2.5 copy-start.5
  256.7 15.1 %collective-permute-start.11 = (f32[256,2,256]{2,0,1:T(8,128)}, f32[256,2,256]{2,0,1:T(8,128)}, u32[]{:S(2)}, u32[]{:S(2)}) collective-permute-start(f32[256,2,256]{2,0,1:T(8,128)} %copy.145), channel_id=1, source_target_pairs={{1,0},{0,1},{3,2},{2,3},{5,4},{4,5},{7,6},{6,7},{9,8},{8,9},{11,10... | collective-permute-start | bytes 1572872 | tf_op jit(solution)/shard_map/ppermute | solution.py:33
  258.2 22.4 %collective-permute-start.10 = (f32[256,2,256]{2,0,1:T(8,128)S(1)}, f32[256,2,256]{2,0,1:T(8,128)S(1)}, u32[]{:S(2)}, u32[]{:S(2)}) collective-permute-start(f32[256,2,256]{2,0,1:T(8,128)S(1)} %copy-done.5), channel_id=1, source_target_pairs={{0,1},{1,0},{2,3},{3,2},{4,5},{5,4},{6,7},{7,6},{8,9},{9,8},{10,11... | collective-permute-start | bytes 1572872 | tf_op jit(solution)/shard_map/ppermute | solution.py:32
  290.1 20.5 %copy-start.21 = (f32[16]{0:T(128)S(1)}, f32[16]{0:T(128)}, u32[]{:S(2)}) copy-start(f32[16]{0:T(128)} %multiply_add_fusion.9) | copy-start | bytes 196
  290.1 21.4 %copy-start.7 = (f32[256]{0:T(256)S(1)}, f32[256]{0:T(256)}, u32[]{:S(2)}) copy-start(f32[256]{0:T(256)} %fusion.226) | copy-start | bytes 3076
